TPU v7x, 512 devices: a whole 4x4x16 slice. The times are simulated.
512 devices in a mesh: dom: 128 (over x, z, core), sub: 4 (over y).
Axes of the slice: x: 4, y: 4, z: 16, core: 2. Of those that a mesh axis runs over, the one named last changes fastest.
Arguments:
- fine_residual: float32 [35, 5, 131072], P(None, None, ('dom', 'sub')), may hold values from -6 to 6
- fine_basis: float32 [64, 35], replicated, may hold values from -1 to 1
- coarse_basis: float32 [64, 10, 131072], P(None, None, ('dom', 'sub')), may hold values from -0.75 to 0.75
- donor_cells: int32 [131072, 4], P(('dom', 'sub')), may hold values from 0 to 65535, as said below
- point_counts: int32 [131072, 4], P(('dom', 'sub')), may hold values from 1 to 32, 64 in all within a row
- solver_pos: int32 [65536], P(('dom', 'sub')), may hold values from 0 to 65535, as said below
- block_inverse: float32 [50, 50, 65536], P(None, None, ('dom', 'sub')), may hold values from -0.25 to 1.65
- face_jacobian: float32 [4, 5, 5, 65536], P(None, None, None, ('dom', 'sub')), may hold values from -0.5 to 0.5
- face_lift: float32 [4, 10, 10], replicated, may hold values from -2 to 2
- face_offset: int32 [4, 65536], P(None, ('dom', 'sub')), may hold values from -32 to 32, as said below
Outputs:
- coarse_residual: float32 [50, 65536], P(None, ('dom', 'sub'))
- correction: float32 [50, 65536], P(None, ('dom', 'sub'))
Inputs may be any that keep to these rules, and one draw needn't show every extreme that they name: `donor_cells`: among the 4 donors of the 256 fine elements of one device, at most 4 lie in any one block of 128 consecutive coarse elements; in 4 groups of 4 consecutive blocks every block receives exactly 4 from every device. `solver_pos`: A permutation; all 128 elements of one block go to one block of 128 solver positions in the same group of 4 consecutive blocks, distinct blocks to distinct ones. `face_offset`: 0 marks a boundary face, and so does a neighbour position outside 0 to 65535.
All inputs are finite; a program needn't handle non-finite values.
Results may differ from a plain program's by a relative error of at most 0.0003.
Values sent between devices are 32-bit elements; how exact they have to be, the bound alone decides.
A program may use at most 64 MiB of HBM per device.

v0:
```python
import functools

import jax
import jax.numpy as jnp
from jax import lax
from jax.experimental import pallas as pl
from jax.experimental.pallas import tpu as pltpu
from jax.sharding import PartitionSpec as P

MESH = pl.DeviceIdType.MESH
F32 = jnp.float32
BF16 = jnp.bfloat16

NZ = 16
NP = 32
NY = 4
ROWS = 56
PIECES = ((0, 32), (32, 24))


def halves(value):
    high = value.astype(BF16)
    return high, (value - high.astype(F32)).astype(BF16)


def dot_nt(left, right):
    return lax.dot_general(left, right, (((1,), (1,)), ((), ())), preferred_element_type=F32)


def dot_nn(left, right):
    return lax.dot_general(left, right, (((1,), (0,)), ((), ())), preferred_element_type=F32)


def ones_where(mask):
    return jnp.where(mask, F32(1.0), F32(0.0))


def iota(shape, dim):
    return lax.broadcasted_iota(jnp.int32, shape, dim)


def kernel(
    residual_hbm,
    fine_basis,
    basis_hbm,
    donors,
    counts,
    positions,
    inverse_hbm,
    jacobian,
    lift,
    offsets,
    coarse_out,
    correction_out,
    residual,
    basis,
    inverse,
    masked,
    pair,
    spread,
    outbox,
    inbox,
    chunks,
    ring_up,
    ring_down,
    group,
    group_pos,
    seats_to_pos,
    chooser,
    lift_rows,
    iterate,
    halo_low,
    halo_high,
    coupling,
    load_sem,
    plane_send,
    plane_recv,
    up_send,
    up_recv,
    down_send,
    down_recv,
    group_send,
    group_recv,
    pos_send,
    pos_recv,
    halo_send,
    halo_recv,
):
    dom = lax.axis_index("dom")
    y = lax.axis_index("sub")
    x = lax.div(dom, 32)
    z = lax.rem(lax.div(dom, 2), NZ)
    core = lax.rem(dom, 2)
    me = x * 8 + core * 4 + y
    block = dom * NY + y

    def plane_peer(step):
        other = lax.rem(me + step, NP)
        far_x = lax.div(other, 8)
        far_core = lax.rem(lax.div(other, 4), 2)
        return ((far_x * NZ + z) * 2 + far_core, lax.rem(other, NY))

    def ring_peer(step):
        return ((x * NZ + lax.rem(z + step, NZ)) * 2 + core, y)

    def group_peer(step):
        return (dom, lax.rem(y + step, NY))

    def line_peer(step):
        other = lax.rem(block + step, 512)
        return (lax.div(other, NY), lax.rem(other, NY))

    load_residual = pltpu.make_async_copy(residual_hbm, residual, load_sem.at[0])
    load_basis = pltpu.make_async_copy(basis_hbm, basis, load_sem.at[1])
    load_inverse = pltpu.make_async_copy(inverse_hbm, inverse, load_sem.at[2])
    load_residual.start()
    load_basis.start()
    load_inverse.start()

    barrier = pltpu.get_barrier_semaphore()

    def greet(step, carry):
        pl.semaphore_signal(barrier, inc=1, device_id=plane_peer(step), device_id_type=MESH)
        return carry

    lax.fori_loop(1, NP, greet, 0)
    for peer in (ring_peer(1), ring_peer(NZ - 1), line_peer(1), line_peer(511)):
        pl.semaphore_signal(barrier, inc=1, device_id=peer, device_id_type=MESH)

    donor_row = jnp.concatenate([donors[k : k + 1, :] for k in range(4)], axis=1)
    owner = lax.shift_right_logical(donor_row, 7)
    seat = jnp.bitwise_and(donor_row, 127).astype(F32)
    owner_f = owner.astype(F32)
    columns = []
    for tile in range(8):
        row = owner_f[:, tile * 128 : (tile + 1) * 128]
        columns.append(jnp.broadcast_to(row, (128, 128)).T)
    earlier = iota((128, 128), 0) < iota((128, 128), 1)
    ranks = []
    for tile in range(8):
        row = owner_f[:, tile * 128 : (tile + 1) * 128]
        total = ones_where((columns[tile] == row) & earlier)
        for before in range(tile):
            total = total + ones_where(columns[before] == row)
        ranks.append(jnp.sum(total, axis=0, keepdims=True))
    rank = jnp.concatenate(ranks, axis=1).astype(jnp.int32)
    far_plane = lax.shift_right_logical(owner, 7) * 8 + jnp.bitwise_and(owner, 7)
    far_z = jnp.bitwise_and(lax.shift_right_logical(owner, 3), 15)
    plane_step = jnp.bitwise_and(far_plane - me + NP, NP - 1)
    order = jnp.bitwise_and(far_z - z + 11 + NZ, NZ - 1)
    slot = plane_step * 32 + lax.shift_right_logical(order, 1) * 4 + rank
    odd = jnp.bitwise_and(order, 1)
    slot_even = jnp.where(odd == 0, slot, -1)
    slot_odd = jnp.where(odd == 1, slot, -1)

    upper0 = counts[0:1, :]
    upper1 = upper0 + counts[1:2, :]
    upper2 = upper1 + counts[2:3, :]
    point = iota((64, 256), 0)
    inside = (
        point < upper0,
        (point >= upper0) & (point < upper1),
        (point >= upper1) & (point < upper2),
        point >= upper2,
    )
    spans = ((0, 32), (0, 64), (0, 64), (32, 64))
    load_residual.wait()
    fine = fine_basis[...].T
    for v in range(5):
        values = lax.dot_general(
            fine,
            residual[v],
            (((1,), (0,)), ((), ())),
            precision=lax.Precision.HIGHEST,
            preferred_element_type=F32,
        )
        for k in range(4):
            masked[k, v] = jnp.where(inside[k], values, F32(0.0))
    load_basis.wait()
    for a in range(10):
        for k in range(4):
            low, high = spans[k]
            product = basis[a, low:high, :][None] * masked[k, :, low:high, :]
            pair[a * 5 : a * 5 + 5, k * 256 : (k + 1) * 256] = jnp.sum(product, axis=1)
    pair[50:51, :] = seat
    pair[51:64, :] = jnp.zeros((13, 1024), F32)
    pair_high, pair_low = halves(pair[...])
    nothing = jnp.zeros((64, 1024), BF16)
    spread[0] = jnp.concatenate([pair_high, nothing, pair_low, nothing], axis=0)
    spread[1] = jnp.concatenate([nothing, pair_high, nothing, pair_low], axis=0)

    pl.semaphore_wait(barrier, 35)

    group_pos[0] = jnp.broadcast_to(positions[...], (8, 128))

    def pos_copy(step):
        return pltpu.make_async_remote_copy(
            src_ref=group_pos.at[0],
            dst_ref=group_pos.at[step],
            send_sem=pos_send.at[step],
            recv_sem=pos_recv.at[step],
            device_id=group_peer(step),
            device_id_type=MESH,
        )

    for step in range(1, NY):
        pos_copy(step).start()

    def plane_copy(half, step):
        return pltpu.make_async_remote_copy(
            src_ref=outbox.at[step, pl.ds(half * 2, 2)],
            dst_ref=inbox.at[pl.ds(half * 2, 2), step],
            send_sem=plane_send.at[half, step],
            recv_sem=plane_recv.at[half, step],
            device_id=plane_peer(step),
            device_id_type=MESH,
        )

    def start_plane(half):
        def body(step, carry):
            plane_copy(half, step).start()
            return carry

        return body

    for part in range(4):
        slots = iota((256, 1024), 0) + part * 256
        rows = dot_nt(ones_where(slots == slot_even).astype(BF16), spread[0])
        rows = rows + dot_nt(ones_where(slots == slot_odd).astype(BF16), spread[1])
        rows = rows[:, :128] + rows[:, 128:]
        outbox[part * 8 : (part + 1) * 8] = rows.reshape(8, 4, 8, 128)
        lax.fori_loop(max(1, part * 8), part * 8 + 8, start_plane(0), 0)
    lax.fori_loop(1, NP, start_plane(1), 0)
    inbox[:, 0] = outbox[0]

    for half in range(3):
        source = iota((128, 128), 0) + half * 128
        for f in range(4):
            offset = offsets[f : f + 1, :]
            own = iota((1, 128), 1)
            there = block * 128 + own + offset
            good = (offset != 0) & (there >= 0) & (there < 65536)
            wanted = jnp.where(good, own + offset + 128, -1)
            chooser[half * 128 : half * 128 + 128, f * 128 : f * 128 + 128] = ones_where(
                source == wanted
            ).astype(BF16)
    row_v = lax.shift_right_logical(iota((80, 64), 0), 4)
    col = iota((80, 64), 1)
    fifth = jnp.zeros((80, 64), jnp.int32)
    for b in range(1, 10):
        fifth = fifth + jnp.where(col >= b * 5, 1, 0)
    same = (col - fifth * 5 == row_v) & (col < 50)
    take_a = ones_where(
        jnp.bitwise_and(iota((80, 10), 0), 15) == iota((80, 10), 1)
    ).astype(BF16)
    b_low = iota((10, 64), 0) * 5
    b_col = iota((10, 64), 1)
    take_b = ones_where((b_col >= b_low) & (b_col < b_low + 5)).astype(BF16)
    for f in range(4):
        for n, part in enumerate(halves(lift[:, f, :])):
            wide = dot_nn(dot_nn(take_a, part).astype(BF16), take_b)
            wide = jnp.where(same, wide, F32(0.0)).astype(BF16)
            lift_rows[f, n * 80 : n * 80 + 80, :] = jnp.concatenate([wide, wide], axis=1)
    for it in range(2):
        iterate[it, 48:64, :] = jnp.zeros((16, 128), F32)
    for step in range(1, NY):
        pos_copy(step).wait_recv()
    place = iota((128, 128), 0) + block * 128
    for step in range(NY):
        seats_to_pos[:, step * 128 : step * 128 + 128] = ones_where(
            place == group_pos[step, 0:1, :]
        ).astype(BF16)

    def wait_plane(half):
        def body(step, carry):
            plane_copy(half, step).wait_recv()
            return carry

        lax.fori_loop(1, NP, body, 0)

    in_pair = jnp.bitwise_and(lax.shift_right_logical(iota((128, 256), 1), 2), 1)
    cell = iota((128, 256), 0).astype(F32)

    def gather(quarter):
        turned = inbox[quarter].reshape(256, 128).T
        high, low = halves(turned)
        for h in range(2):
            left = jnp.concatenate(
                [high[h * 64 : h * 64 + 64], low[h * 64 : h * 64 + 64]], axis=0
            )
            hit = cell == turned[h * 64 + 50 : h * 64 + 51, :]
            right = jnp.concatenate(
                [
                    ones_where(hit & (in_pair == 0)).astype(BF16),
                    ones_where(hit & (in_pair == 1)).astype(BF16),
                ],
                axis=0,
            )
            both = dot_nt(left, right)
            both = both[:64] + both[64:]
            for n in range(2):
                chunks[quarter * 4 + n * 2 + h] = both[:, n * 128 : n * 128 + 128]

    def chunk_of(relative):
        return (relative + 11) % 16

    def ring_copy(s, piece, up):
        start, size = PIECES[piece]
        relative = 8 - s if up else s - 7
        return pltpu.make_async_remote_copy(
            src_ref=chunks.at[chunk_of(relative), pl.ds(start, size)],
            dst_ref=(ring_up if up else ring_down).at[s, pl.ds(start, size)],
            send_sem=(up_send if up else down_send).at[s, piece],
            recv_sem=(up_recv if up else down_recv).at[s, piece],
            device_id=ring_peer(1 if up else NZ - 1),
            device_id_type=MESH,
        )

    wait_plane(0)
    gather(0)
    gather(1)
    for s in range(8):
        for piece, (start, size) in enumerate(PIECES):
            for up in (True, False):
                if not up and s == 7:
                    continue
                if s:
                    ring_copy(s - 1, piece, up).wait_recv()
                    index = chunk_of(8 - s if up else s - 7)
                    arrived = (ring_up if up else ring_down)[s - 1, start : start + size, :]
                    chunks[index, start : start + size, :] += arrived
                ring_copy(s, piece, up).start()
        if s == 2:
            wait_plane(1)
            gather(2)
        if s == 3:
            gather(3)

    def group_copy(step, piece):
        start, size = PIECES[piece]
        return pltpu.make_async_remote_copy(
            src_ref=group.at[0, pl.ds(start, size)],
            dst_ref=group.at[step, pl.ds(start, size)],
            send_sem=group_send.at[step, piece],
            recv_sem=group_recv.at[step, piece],
            device_id=group_peer(step),
            device_id_type=MESH,
        )

    for piece, (start, size) in enumerate(PIECES):
        ring_copy(6, piece, False).wait_recv()
        mine = chunks[chunk_of(0), start : start + size, :] + ring_down[6, start : start + size, :]
        ring_copy(7, piece, True).wait_recv()
        group[0, start : start + size, :] = mine + ring_up[7, start : start + size, :]
        for step in range(1, NY):
            group_copy(step, piece).start()
    load_inverse.wait()
    for piece in range(len(PIECES)):
        for step in range(1, NY):
            group_copy(step, piece).wait_recv()
    blank = jnp.zeros((8, 128), F32)
    wide = jnp.concatenate(
        [jnp.concatenate([group[step], blank], axis=0) for step in range(NY)], axis=1
    )
    high, low = halves(wide)
    coarse = dot_nt(jnp.concatenate([high, low], axis=0), seats_to_pos[...])
    coarse = (coarse[:64] + coarse[64:])[:50]
    coarse_out[...] = coarse

    def apply_inverse(field):
        return jnp.sum(inverse[...] * field[None], axis=1)

    def halo_copy(it, up):
        return pltpu.make_async_remote_copy(
            src_ref=iterate.at[it, pl.ds(0, ROWS)],
            dst_ref=(halo_low if up else halo_high).at[it],
            send_sem=halo_send.at[it, 0 if up else 1],
            recv_sem=halo_recv.at[it, 0 if up else 1],
            device_id=line_peer(1 if up else 511),
            device_id_type=MESH,
        )

    field = apply_inverse(coarse)
    for it in range(2):
        iterate[it, 0:50, :] = field
        halo_copy(it, True).start()
        halo_copy(it, False).start()
        halo_copy(it, True).wait_recv()
        halo_copy(it, False).wait_recv()
        wide = jnp.concatenate(
            [
                jnp.concatenate([halo_low[it], blank], axis=0),
                iterate[it],
                jnp.concatenate([halo_high[it], blank], axis=0),
            ],
            axis=1,
        )
        high, low = halves(wide)
        picked = dot_nn(jnp.concatenate([high, low], axis=0), chooser[...]).astype(BF16)
        lifted = []
        for f in range(4):
            both = dot_nn(lift_rows[f], picked[:, f * 128 : f * 128 + 128])
            lifted.append(both[:80] + both[80:])
        for w in range(5):
            total = jnp.zeros((16, 128), F32)
            for f in range(4):
                for v in range(5):
                    total = total + lifted[f][v * 16 : v * 16 + 16] * jacobian[w, v, f : f + 1, :]
            coupling[pl.ds(w, 10, stride=5), :] = total[:10]
        field = apply_inverse(coarse - coupling[0:50, :])
    correction_out[...] = field

    for half in range(2):

        def sent(step, carry, half=half):
            plane_copy(half, step).wait_send()
            return carry

        lax.fori_loop(1, NP, sent, 0)
    for s in range(8):
        for piece in range(len(PIECES)):
            ring_copy(s, piece, True).wait_send()
            if s < 7:
                ring_copy(s, piece, False).wait_send()
    for step in range(1, NY):
        pos_copy(step).wait_send()
        for piece in range(len(PIECES)):
            group_copy(step, piece).wait_send()
    for it in range(2):
        halo_copy(it, True).wait_send()
        halo_copy(it, False).wait_send()


def per_device(
    fine_residual,
    fine_basis,
    coarse_basis,
    donor_cells,
    point_counts,
    solver_pos,
    block_inverse,
    face_jacobian,
    face_lift,
    face_offset,
):
    vmem = pl.BlockSpec(memory_space=pltpu.VMEM)
    hbm = pl.BlockSpec(memory_space=pl.ANY)
    pieces = len(PIECES)
    dma = pltpu.SemaphoreType.DMA
    return pl.pallas_call(
        kernel,
        out_shape=(
            jax.ShapeDtypeStruct((50, 128), F32),
            jax.ShapeDtypeStruct((50, 128), F32),
        ),
        in_specs=[hbm, vmem, hbm, vmem, vmem, vmem, hbm, vmem, vmem, vmem],
        out_specs=(vmem, vmem),
        scratch_shapes=[
            pltpu.VMEM((5, 35, 256), F32),
            pltpu.VMEM((10, 64, 256), F32),
            pltpu.VMEM((50, 50, 128), F32),
            pltpu.VMEM((4, 5, 64, 256), F32),
            pltpu.VMEM((64, 1024), F32),
            pltpu.VMEM((2, 256, 1024), BF16),
            pltpu.VMEM((NP, 4, 8, 128), F32),
            pltpu.VMEM((4, NP, 8, 128), F32),
            pltpu.VMEM((NZ, 64, 128), F32),
            pltpu.VMEM((8, ROWS, 128), F32),
            pltpu.VMEM((7, ROWS, 128), F32),
            pltpu.VMEM((NY, ROWS, 128), F32),
            pltpu.VMEM((NY, 8, 128), jnp.int32),
            pltpu.VMEM((128, 512), BF16),
            pltpu.VMEM((384, 512), BF16),
            pltpu.VMEM((4, 160, 128), BF16),
            pltpu.VMEM((2, 64, 128), F32),
            pltpu.VMEM((2, ROWS, 128), F32),
            pltpu.VMEM((2, ROWS, 128), F32),
            pltpu.VMEM((64, 128), F32),
            dma((3,)),
            dma((2, NP)),
            dma((2, NP)),
            dma((8, pieces)),
            dma((8, pieces)),
            dma((7, pieces)),
            dma((7, pieces)),
            dma((NY, pieces)),
            dma((NY, pieces)),
            dma((NY,)),
            dma((NY,)),
            dma((2, 2)),
            dma((2, 2)),
        ],
        compiler_params=pltpu.CompilerParams(
            collective_id=0, has_side_effects=True, vmem_limit_bytes=40 * 1024 * 1024
        ),
    )(
        fine_residual.transpose(1, 0, 2),
        fine_basis.T,
        coarse_basis.transpose(1, 0, 2),
        donor_cells.T,
        point_counts.T,
        solver_pos.reshape(1, 128),
        block_inverse,
        face_jacobian.transpose(1, 2, 0, 3),
        face_lift.transpose(1, 0, 2),
        face_offset,
    )


def solution(mesh):
    in_specs = (
        P(None, None, ("dom", "sub")),
        P(),
        P(None, None, ("dom", "sub")),
        P(("dom", "sub"), None),
        P(("dom", "sub"), None),
        P(("dom", "sub")),
        P(None, None, ("dom", "sub")),
        P(None, None, None, ("dom", "sub")),
        P(),
        P(None, ("dom", "sub")),
    )
    out_specs = (P(None, ("dom", "sub")), P(None, ("dom", "sub")))
    return jax.shard_map(
        per_device, mesh=mesh, in_specs=in_specs, out_specs=out_specs, check_vma=False
    )
```

profile of v0, /device:TPU:6, one launch (start us, length us, event | category | flops | bytes accessed | tf_op | source)
XLA Modules:
  0.0 75.1 jit_solution(15014743409442163445)
XLA Ops:
  0.6 0.0 copy-start
  0.6 1.4 %copy-done = f32[50,50,128]{2,1,0:T(8,128)S(1)} copy-done((f32[50,50,128]{2,1,0:T(8,128)S(1)}, f32[50,50,128]{2,1,0:T(8,128)}, u32[]{:S(2)}) %copy-start) | copy-done | bytes 1280024
  2.0 0.0 copy-start.1
  2.0 1.1 %copy-done.1 = f32[64,10,256]{2,0,1:T(8,128)S(1)} copy-done((f32[64,10,256]{2,0,1:T(8,128)S(1)}, f32[64,10,256]{2,0,1:T(8,128)}, u32[]{:S(2)}) %copy-start.1) | copy-done | bytes 655384
  3.1 0.0 copy-start.2
  3.1 0.9 %copy-done.2 = f32[35,5,256]{2,0,1:T(8,128)S(1)} copy-done((f32[35,5,256]{2,0,1:T(8,128)S(1)}, f32[35,5,256]{2,0,1:T(8,128)}, u32[]{:S(2)}) %copy-start.2) | copy-done | bytes 179224
  4.0 0.0 copy-start.3
  4.0 0.8 %copy-done.3 = f32[4,5,5,128]{3,0,2,1:T(4,128)S(1)} copy-done((f32[4,5,5,128]{3,0,2,1:T(4,128)S(1)}, f32[4,5,5,128]{3,0,2,1:T(4,128)}, u32[]{:S(2)}) %copy-start.3) | copy-done | bytes 51224
  4.8 0.0 copy-start.4
  4.8 0.7 copy-done.4
  5.5 0.0 copy-start.5
  5.5 0.7 copy-done.5
  6.3 0.0 copy-start.6
  6.3 0.7 copy-done.6
  7.0 0.0 copy-start.7
  7.0 0.7 copy-done.7
  7.6 0.0 copy-start.8
  7.6 0.7 copy-done.8
  8.3 0.0 copy-start.9
  8.3 0.7 copy-done.9
  9.0 64.9 %shard_map.113 = (f32[50,128]{1,0:T(8,128)S(1)}, f32[50,128]{1,0:T(8,128)S(1)}) custom-call(f32[5,35,256]{2,1,0:T(8,128)S(1)} %bitcast.9, f32[35,64]{1,0:T(8,128)S(1)} %bitcast.11, f32[10,64,256]{2,1,0:T(8,128)S(1)} %bitcast.8, s32[4,256]{1,0:T(4,128)S(1)} %bitcast.13, s32[4,256]{1,0:T(4,128)S(1)} %bitcast.14, s32[1,128]{1,0:T(1,128)S(1)} %bitcast.15, ...), custom_call_target="tpu_custom_call" | custom-call | tf_op jit(solution)/shard_map/pallas_call | solution.py:450
  73.9 0.6 copy.14
  74.5 0.6 copy.15
Async XLA Ops:
  0.6 1.4 %copy-start = (f32[50,50,128]{2,1,0:T(8,128)S(1)}, f32[50,50,128]{2,1,0:T(8,128)}, u32[]{:S(2)}) copy-start(f32[50,50,128]{2,1,0:T(8,128)} %inverse_hbm.1) | copy-start | bytes 3840004
  2.0 1.1 %copy-start.1 = (f32[64,10,256]{2,0,1:T(8,128)S(1)}, f32[64,10,256]{2,0,1:T(8,128)}, u32[]{:S(2)}) copy-start(f32[64,10,256]{2,0,1:T(8,128)} %param.12) | copy-start | bytes 1966084
  3.1 0.9 %copy-start.2 = (f32[35,5,256]{2,0,1:T(8,128)S(1)}, f32[35,5,256]{2,0,1:T(8,128)}, u32[]{:S(2)}) copy-start(f32[35,5,256]{2,0,1:T(8,128)} %param.10) | copy-start | bytes 537604
  4.0 0.8 %copy-start.3 = (f32[4,5,5,128]{3,0,2,1:T(4,128)S(1)}, f32[4,5,5,128]{3,0,2,1:T(4,128)}, u32[]{:S(2)}) copy-start(f32[4,5,5,128]{3,0,2,1:T(4,128)} %param.17) | copy-start | bytes 153604
  4.8 0.7 copy-start.4
  5.5 0.7 copy-start.5
  6.3 0.7 copy-start.6
  7.0 0.7 copy-start.7
  7.6 0.7 copy-start.8
  8.3 0.7 copy-start.9
where the time goes:
time: 75.6 us; the launch traced here: 75.1 us
  Pallas kernels  64.9 us (86%)
  local copies, waits for them, and re-layouts  9.55 us (13%)
    pallas_call x1, Pallas kernels, per_device(): pl.pallas_call(kernel, out_shape=(jax.ShapeDtypeStruct((50, 128), F32), j...  64.9 us
    unnamed x22, local copies, waits for them, and re-layouts  9.55 us

commit v1 on v0

v1 whole, which is shorter than its diff:
```python
import functools

import jax
import jax.numpy as jnp
from jax import lax
from jax.experimental import pallas as pl
from jax.experimental.pallas import tpu as pltpu
from jax.sharding import PartitionSpec as P

MESH = pl.DeviceIdType.MESH
F32 = jnp.float32
BF16 = jnp.bfloat16

NZ = 16
NP = 32
NY = 4
ROWS = 56
PARTS = (2, 1, 3, 0)
VIA = ((3, 8), (-3, -7), (2, 7), (-2, -6), (1, 6), (-1, -5))
LAST = (4, -3, 3, -2, 2, -1, 1, 5, -4)


def halves(value):
    high = value.astype(BF16)
    return high, (value - high.astype(F32)).astype(BF16)


def dot_nt(left, right):
    return lax.dot_general(left, right, (((1,), (1,)), ((), ())), preferred_element_type=F32)


def dot_nn(left, right):
    return lax.dot_general(left, right, (((1,), (0,)), ((), ())), preferred_element_type=F32)


def ones_where(mask):
    return jnp.where(mask, F32(1.0), F32(0.0))


def iota(shape, dim):
    return lax.broadcasted_iota(jnp.int32, shape, dim)


def kernel(
    residual_hbm,
    fine_basis_hbm,
    basis_hbm,
    donors_hbm,
    counts_hbm,
    positions_hbm,
    inverse_hbm,
    jacobian_hbm,
    lift_hbm,
    offsets_hbm,
    coarse_out,
    correction_out,
    residual,
    fine_basis,
    basis,
    donors,
    counts,
    positions,
    inverse,
    jacobian,
    lift,
    offsets,
    masked,
    pair,
    spread,
    outbox,
    inbox,
    chunks,
    via_in,
    last_in,
    group,
    group_pos,
    seats_to_pos,
    chooser,
    lift_rows,
    ends_high,
    ends_low,
    halo_low,
    halo_high,
    coupling,
    load_sem,
    plane_send,
    plane_recv,
    via_send,
    via_recv,
    last_send,
    last_recv,
    group_send,
    group_recv,
    pos_send,
    pos_recv,
    halo_send,
    halo_recv,
):
    dom = lax.axis_index("dom")
    y = lax.axis_index("sub")
    x = lax.div(dom, 32)
    z = lax.rem(lax.div(dom, 2), NZ)
    core = lax.rem(dom, 2)
    block = dom * NY + y

    def plane_peer(step):
        far_x = lax.rem(x + lax.div(step, 8), 4)
        far_core = lax.rem(core + lax.div(step, 4), 2)
        far_y = lax.rem(y + step, NY)
        return ((far_x * NZ + z) * 2 + far_core, far_y)

    def ring_peer(step):
        return ((x * NZ + lax.rem(z + step, NZ)) * 2 + core, y)

    def group_peer(step):
        return (dom, lax.rem(y + step, NY))

    def line_peer(step):
        other = lax.rem(block + step, 512)
        return (lax.div(other, NY), lax.rem(other, NY))

    loads = [
        pltpu.make_async_copy(source, target, load_sem.at[n])
        for n, (source, target) in enumerate(
            (
                (donors_hbm, donors),
                (counts_hbm, counts),
                (fine_basis_hbm, fine_basis),
                (residual_hbm, residual),
                (basis_hbm, basis),
                (positions_hbm, positions),
                (offsets_hbm, offsets),
                (lift_hbm, lift),
                (jacobian_hbm, jacobian),
                (inverse_hbm, inverse),
            )
        )
    ]
    for load in loads:
        load.start()

    barrier = pltpu.get_barrier_semaphore()

    for step in (5, 11, 4, 12, 3, 13, 2, 14, 1, 15):
        pl.semaphore_signal(barrier, inc=1, device_id=ring_peer(step), device_id_type=MESH)

    def plane_steps(part, body):
        def turned(i, carry):
            body(part * 8 + lax.rem(i, 2) * 4 + lax.rem(2 + 3 * lax.div(i, 2), NY))
            return carry

        def near(step, carry):
            body(step)
            return carry

        if part:
            lax.fori_loop(0, 8, turned, 0)
        else:
            lax.fori_loop(1, 8, near, 0)

    def greet(step):
        pl.semaphore_signal(barrier, inc=1, device_id=plane_peer(step), device_id_type=MESH)

    for part in PARTS:
        plane_steps(part, greet)
    for step in (1, 511):
        pl.semaphore_signal(barrier, inc=1, device_id=line_peer(step), device_id_type=MESH)

    loads[0].wait()
    donor_row = jnp.concatenate([donors[k : k + 1, :] for k in range(4)], axis=1)
    owner = lax.shift_right_logical(donor_row, 7)
    seat = jnp.bitwise_and(donor_row, 127).astype(F32)
    owner_f = owner.astype(F32)
    columns = []
    for tile in range(8):
        row = owner_f[:, tile * 128 : (tile + 1) * 128]
        columns.append(jnp.broadcast_to(row, (128, 128)).T)
    earlier = iota((128, 128), 0) < iota((128, 128), 1)
    ranks = []
    for tile in range(8):
        row = owner_f[:, tile * 128 : (tile + 1) * 128]
        total = ones_where((columns[tile] == row) & earlier)
        for before in range(tile):
            total = total + ones_where(columns[before] == row)
        ranks.append(jnp.sum(total, axis=0, keepdims=True))
    rank = jnp.concatenate(ranks, axis=1).astype(jnp.int32)
    far_z = jnp.bitwise_and(lax.shift_right_logical(owner, 3), 15)
    step_x = jnp.bitwise_and(lax.shift_right_logical(owner, 7) - x + 4, 3)
    step_core = jnp.bitwise_and(lax.shift_right_logical(owner, 2) - core + 2, 1)
    step_y = jnp.bitwise_and(owner - y + 4, 3)
    plane_step = step_x * 8 + step_core * 4 + step_y
    order = jnp.bitwise_and(far_z - z + 11 + NZ, NZ - 1)
    slot = plane_step * 32 + lax.shift_right_logical(order, 1) * 4 + rank
    odd = jnp.bitwise_and(order, 1)
    slot_even = jnp.where(odd == 0, slot, -1)
    slot_odd = jnp.where(odd == 1, slot, -1)

    for load in loads[1:4]:
        load.wait()
    upper0 = counts[0:1, :]
    upper1 = upper0 + counts[1:2, :]
    upper2 = upper1 + counts[2:3, :]
    point = iota((64, 256), 0)
    inside = (
        point < upper0,
        (point >= upper0) & (point < upper1),
        (point >= upper1) & (point < upper2),
        point >= upper2,
    )
    spans = ((0, 32), (0, 64), (0, 64), (32, 64))
    fine = fine_basis[...].T
    for v in range(5):
        values = lax.dot_general(
            fine,
            residual[v],
            (((1,), (0,)), ((), ())),
            precision=lax.Precision.HIGHEST,
            preferred_element_type=F32,
        )
        for k in range(4):
            masked[k, v] = jnp.where(inside[k], values, F32(0.0))
    loads[4].wait()
    for a in range(10):
        for k in range(4):
            low, high = spans[k]
            product = basis[a, low:high, :][None] * masked[k, :, low:high, :]
            pair[a * 5 : a * 5 + 5, k * 256 : (k + 1) * 256] = jnp.sum(product, axis=1)
    pair[50:51, :] = seat
    pair[51:64, :] = jnp.zeros((13, 1024), F32)
    pair_high, pair_low = halves(pair[...])
    nothing = jnp.zeros((64, 1024), BF16)
    spread[0] = jnp.concatenate([pair_high, nothing, pair_low, nothing], axis=0)
    spread[1] = jnp.concatenate([nothing, pair_high, nothing, pair_low], axis=0)

    for part in PARTS:
        slots = iota((256, 1024), 0) + part * 256
        rows = dot_nt(ones_where(slots == slot_even).astype(BF16), spread[0])
        rows = rows + dot_nt(ones_where(slots == slot_odd).astype(BF16), spread[1])
        rows = rows[:, :128] + rows[:, 128:]
        outbox[part * 8 : (part + 1) * 8] = rows.reshape(8, 4, 8, 128)

    pl.semaphore_wait(barrier, 43)
    loads[5].wait()

    group_pos[0] = jnp.broadcast_to(positions[...], (8, 128))

    def pos_copy(step):
        return pltpu.make_async_remote_copy(
            src_ref=group_pos.at[0],
            dst_ref=group_pos.at[step],
            send_sem=pos_send.at[step],
            recv_sem=pos_recv.at[step],
            device_id=group_peer(step),
            device_id_type=MESH,
        )

    def plane_copy(half, step):
        return pltpu.make_async_remote_copy(
            src_ref=outbox.at[step, pl.ds(half * 2, 2)],
            dst_ref=inbox.at[pl.ds(half * 2, 2), step],
            send_sem=plane_send.at[half],
            recv_sem=plane_recv.at[half],
            device_id=plane_peer(step),
            device_id_type=MESH,
        )

    for half in range(2):
        for part in PARTS:
            plane_steps(part, lambda step, half=half: plane_copy(half, step).start())
    for step in range(1, NY):
        pos_copy(step).start()
    inbox[:, 0] = outbox[0]

    for load in loads[6:8]:
        load.wait()
    own = iota((1, 128), 1)
    for f in range(4):
        offset = offsets[f : f + 1, :]
        there = block * 128 + own + offset
        good = (offset != 0) & (there >= 0) & (there < 65536)
        near = own + offset
        beyond = jnp.where(near < 0, near + 256, near)
        wanted = jnp.where(good, beyond, -1)
        for half in range(2):
            source = iota((128, 128), 0) + half * 128
            chooser[half * 128 : half * 128 + 128, f * 128 : f * 128 + 128] = ones_where(
                source == wanted
            ).astype(BF16)
    row_v = lax.shift_right_logical(iota((80, 64), 0), 4)
    col = iota((80, 64), 1)
    fifth = jnp.zeros((80, 64), jnp.int32)
    for b in range(1, 10):
        fifth = fifth + jnp.where(col >= b * 5, 1, 0)
    same = (col - fifth * 5 == row_v) & (col < 50)
    take_a = ones_where(
        jnp.bitwise_and(iota((80, 10), 0), 15) == iota((80, 10), 1)
    ).astype(BF16)
    b_low = iota((10, 64), 0) * 5
    b_col = iota((10, 64), 1)
    take_b = ones_where((b_col >= b_low) & (b_col < b_low + 5)).astype(BF16)
    for f in range(4):
        for n, part in enumerate(halves(lift[:, f, :])):
            wide = dot_nn(dot_nn(take_a, part).astype(BF16), take_b)
            wide = jnp.where(same, wide, F32(0.0)).astype(BF16)
            lift_rows[f, n * 80 : n * 80 + 80, :] = jnp.concatenate([wide, wide], axis=1)
    for step in range(1, NY):
        pos_copy(step).wait_recv()
    place = iota((128, 128), 0) + block * 128
    for step in range(NY):
        seats_to_pos[:, step * 128 : step * 128 + 128] = ones_where(
            place == group_pos[step, 0:1, :]
        ).astype(BF16)

    def wait_plane(half, sems):
        whole = inbox.at[pl.ds(half * 2, 2), pl.ds(1, NP - 1)]
        pltpu.make_async_copy(whole, whole, sems.at[half]).wait()

    in_pair = jnp.bitwise_and(lax.shift_right_logical(iota((128, 256), 1), 2), 1)
    cell = iota((128, 256), 0).astype(F32)

    def gather(quarter):
        turned = inbox[quarter].reshape(256, 128).T
        high, low = halves(turned)
        for h in range(2):
            left = jnp.concatenate(
                [high[h * 64 : h * 64 + 64], low[h * 64 : h * 64 + 64]], axis=0
            )
            hit = cell == turned[h * 64 + 50 : h * 64 + 51, :]
            right = jnp.concatenate(
                [
                    ones_where(hit & (in_pair == 0)).astype(BF16),
                    ones_where(hit & (in_pair == 1)).astype(BF16),
                ],
                axis=0,
            )
            both = dot_nt(left, right)
            both = both[:64] + both[64:]
            for n in range(2):
                chunks[quarter * 4 + n * 2 + h] = both[:, n * 128 : n * 128 + 128]

    def chunk_of(relative):
        return (relative + 11) % 16

    def via_copy(n):
        step, relative = VIA[n]
        return pltpu.make_async_remote_copy(
            src_ref=chunks.at[chunk_of(relative), pl.ds(0, ROWS)],
            dst_ref=via_in.at[n],
            send_sem=via_send.at[n],
            recv_sem=via_recv.at[n],
            device_id=ring_peer(step % NZ),
            device_id_type=MESH,
        )

    def last_copy(n):
        relative = LAST[n]
        return pltpu.make_async_remote_copy(
            src_ref=chunks.at[chunk_of(relative), pl.ds(0, ROWS)],
            dst_ref=last_in.at[n],
            send_sem=last_send.at[n],
            recv_sem=last_recv.at[n],
            device_id=ring_peer(relative % NZ),
            device_id_type=MESH,
        )

    wait_plane(0, plane_recv)
    gather(0)
    for n in (0, 2, 4):
        via_copy(n).start()
    gather(1)
    for n in (1, 3, 5):
        via_copy(n).start()
    wait_plane(1, plane_recv)
    gather(2)
    gather(3)
    for n in range(7):
        last_copy(n).start()
    for n in range(6):
        via_copy(n).wait_recv()
    for first, relative in ((0, 5), (1, -4)):
        added = via_in[first] + via_in[first + 2] + via_in[first + 4]
        chunks[chunk_of(relative), 0:ROWS, :] += added
    for n in (7, 8):
        last_copy(n).start()
    def group_copy(step):
        return pltpu.make_async_remote_copy(
            src_ref=group.at[0],
            dst_ref=group.at[step],
            send_sem=group_send.at[step],
            recv_sem=group_recv.at[step],
            device_id=group_peer(step),
            device_id_type=MESH,
        )

    mine = chunks[chunk_of(0), 0:ROWS, :]
    for n in range(9):
        last_copy(n).wait_recv()
        mine = mine + last_in[n]
    group[0] = mine
    for step in (2, 1, 3):
        group_copy(step).start()
    for load in loads[8:]:
        load.wait()
    for step in (1, 3, 2):
        group_copy(step).wait_recv()
    blank = jnp.zeros((8, 128), F32)
    wide = jnp.concatenate(
        [jnp.concatenate([group[step], blank], axis=0) for step in range(NY)], axis=1
    )
    high, low = halves(wide)
    coarse = dot_nt(jnp.concatenate([high, low], axis=0), seats_to_pos[...])
    coarse = (coarse[:64] + coarse[64:])[:50]
    coarse_out[...] = coarse

    def apply_inverse(field):
        return jnp.sum(inverse[...] * field[None], axis=1)

    def halo_copy(it, up):
        return pltpu.make_async_remote_copy(
            src_ref=(ends_high if up else ends_low).at[it],
            dst_ref=(halo_low if up else halo_high).at[it],
            send_sem=halo_send.at[it, 0 if up else 1],
            recv_sem=halo_recv.at[it, 0 if up else 1],
            device_id=line_peer(1 if up else 511),
            device_id_type=MESH,
        )

    lane_part = lax.shift_right_logical(iota((16, 128), 1), 5)

    def packed(rows, from_part):
        total = jnp.zeros((16, 128), F32)
        for g in range(4):
            shift = (g - from_part) % 4 * 32
            group_rows = rows[g * 16 : g * 16 + 16]
            turned = pltpu.roll(group_rows, shift, 1) if shift else group_rows
            total = jnp.where(lane_part == g, turned, total)
        return total

    def unpacked(low_ends, high_ends):
        parts = []
        for g in range(4):
            low_shift = (3 - g) % 4 * 32
            high_shift = (4 - g) % 4 * 32
            low_rows = pltpu.roll(low_ends, low_shift, 1) if low_shift else low_ends
            high_rows = pltpu.roll(high_ends, high_shift, 1) if high_shift else high_ends
            parts.append(jnp.where(lane_part == 3, low_rows, jnp.where(lane_part == 0, high_rows, F32(0.0))))
        return jnp.concatenate(parts, axis=0)

    field = apply_inverse(coarse)
    tail = jnp.zeros((14, 128), F32)
    for it in range(2):
        whole = jnp.concatenate([field, tail], axis=0)
        ends_high[it] = packed(whole, 3)
        ends_low[it] = packed(whole, 0)
        halo_copy(it, True).start()
        halo_copy(it, False).start()
        halo_copy(it, True).wait_recv()
        halo_copy(it, False).wait_recv()
        wide = jnp.concatenate([whole, unpacked(halo_low[it], halo_high[it])], axis=1)
        high, low = halves(wide)
        picked = dot_nn(jnp.concatenate([high, low], axis=0), chooser[...]).astype(BF16)
        lifted = []
        for f in range(4):
            both = dot_nn(lift_rows[f], picked[:, f * 128 : f * 128 + 128])
            lifted.append(both[:80] + both[80:])
        for w in range(5):
            total = jnp.zeros((16, 128), F32)
            for f in range(4):
                for v in range(5):
                    total = total + lifted[f][v * 16 : v * 16 + 16] * jacobian[w, v, f : f + 1, :]
            coupling[pl.ds(w, 10, stride=5), :] = total[:10]
        field = apply_inverse(coarse - coupling[0:50, :])
    correction_out[...] = field

    for half in range(2):
        wait_plane(half, plane_send)
    for n in range(6):
        via_copy(n).wait_send()
    for n in range(9):
        last_copy(n).wait_send()
    for step in range(1, NY):
        pos_copy(step).wait_send()
        group_copy(step).wait_send()
    for it in range(2):
        halo_copy(it, True).wait_send()
        halo_copy(it, False).wait_send()


def per_device(
    fine_residual,
    fine_basis,
    coarse_basis,
    donor_cells,
    point_counts,
    solver_pos,
    block_inverse,
    face_jacobian,
    face_lift,
    face_offset,
):
    vmem = pl.BlockSpec(memory_space=pltpu.VMEM)
    hbm = pl.BlockSpec(memory_space=pl.ANY)
    dma = pltpu.SemaphoreType.DMA
    return pl.pallas_call(
        kernel,
        out_shape=(
            jax.ShapeDtypeStruct((50, 128), F32),
            jax.ShapeDtypeStruct((50, 128), F32),
        ),
        in_specs=[hbm] * 10,
        out_specs=(vmem, vmem),
        scratch_shapes=[
            pltpu.VMEM((5, 35, 256), F32),
            pltpu.VMEM((35, 64), F32),
            pltpu.VMEM((10, 64, 256), F32),
            pltpu.VMEM((4, 256), jnp.int32),
            pltpu.VMEM((4, 256), jnp.int32),
            pltpu.VMEM((1, 128), jnp.int32),
            pltpu.VMEM((50, 50, 128), F32),
            pltpu.VMEM((5, 5, 4, 128), F32),
            pltpu.VMEM((10, 4, 10), F32),
            pltpu.VMEM((4, 128), jnp.int32),
            pltpu.VMEM((4, 5, 64, 256), F32),
            pltpu.VMEM((64, 1024), F32),
            pltpu.VMEM((2, 256, 1024), BF16),
            pltpu.VMEM((NP, 4, 8, 128), F32),
            pltpu.VMEM((4, NP, 8, 128), F32),
            pltpu.VMEM((NZ, 64, 128), F32),
            pltpu.VMEM((6, ROWS, 128), F32),
            pltpu.VMEM((9, ROWS, 128), F32),
            pltpu.VMEM((NY, ROWS, 128), F32),
            pltpu.VMEM((NY, 8, 128), jnp.int32),
            pltpu.VMEM((128, 512), BF16),
            pltpu.VMEM((256, 512), BF16),
            pltpu.VMEM((4, 160, 128), BF16),
            pltpu.VMEM((2, 16, 128), F32),
            pltpu.VMEM((2, 16, 128), F32),
            pltpu.VMEM((2, 16, 128), F32),
            pltpu.VMEM((2, 16, 128), F32),
            pltpu.VMEM((64, 128), F32),
            dma((10,)),
            dma((2,)),
            dma((2,)),
            dma((6,)),
            dma((6,)),
            dma((9,)),
            dma((9,)),
            dma((NY,)),
            dma((NY,)),
            dma((NY,)),
            dma((NY,)),
            dma((2, 2)),
            dma((2, 2)),
        ],
        compiler_params=pltpu.CompilerParams(
            collective_id=0, has_side_effects=True
        ),
    )(
        fine_residual.transpose(1, 0, 2),
        fine_basis.T,
        coarse_basis.transpose(1, 0, 2),
        donor_cells.T,
        point_counts.T,
        solver_pos.reshape(1, 128),
        block_inverse,
        face_jacobian.transpose(1, 2, 0, 3),
        face_lift.transpose(1, 0, 2),
        face_offset,
    )


def solution(mesh):
    in_specs = (
        P(None, None, ("dom", "sub")),
        P(),
        P(None, None, ("dom", "sub")),
        P(("dom", "sub"), None),
        P(("dom", "sub"), None),
        P(("dom", "sub")),
        P(None, None, ("dom", "sub")),
        P(None, None, None, ("dom", "sub")),
        P(),
        P(None, ("dom", "sub")),
    )
    out_specs = (P(None, ("dom", "sub")), P(None, ("dom", "sub")))
    return jax.shard_map(
        per_device, mesh=mesh, in_specs=in_specs, out_specs=out_specs, check_vma=False
    )
```

time: 75.6 us -> 58.3 us (0.77)
  Pallas kernels: 64.9 us -> 54.6 us
  local copies, waits for them, and re-layouts: 9.55 us -> 2.72 us
    pallas_call x1, Pallas kernels: 64.9 us -> 54.6 us  [per_device(): pl.pallas_call(kernel, out_shape=(jax.ShapeDtypeStruct((50, 128), F32), j...]
    unnamed x22 -> x2, local copies, waits for them, and re-layouts: 9.55 us -> 2.72 us
where the time goes in v1:
time: 58.3 us; the launch traced here: 58 us
  Pallas kernels  54.6 us (94%)
  local copies, waits for them, and re-layouts  2.72 us (5%)
  between operations  0.64 us (1%)
    pallas_call x1, Pallas kernels, per_device(): pl.pallas_call(kernel, out_shape=(jax.ShapeDtypeStruct((50, 128), F32), j...  54.6 us
    unnamed x2, local copies, waits for them, and re-layouts  2.72 us

profile of v1, /device:TPU:6, one launch (start us, length us, event | category | flops | bytes accessed | tf_op | source)
XLA Modules:
  0.0 58.0 jit_solution(401811699114566969)
XLA Ops:
  0.6 54.6 %shard_map.113 = (f32[50,128]{1,0:T(8,128)}, f32[50,128]{1,0:T(8,128)}) custom-call(f32[5,35,256]{2,1,0:T(8,128)} %bitcast.9, f32[35,64]{1,0:T(8,128)} %bitcast.11, f32[10,64,256]{2,1,0:T(8,128)} %bitcast.8, s32[4,256]{1,0:T(4,128)} %bitcast.13, s32[4,256]{1,0:T(4,128)} %bitcast.14, s32[1,128]{1,0:T(1,128)} %bitcast.15, f32[50,50,128]{2,1,0:T(8,128)} %inverse_hbm.1, ...), custom_call_target="tpu_custom_call" | custom-call | tf_op jit(solution)/shard_map/pallas_call | solution.py:504
  55.3 1.4 %copy.14 = f32[50,128]{1,0:T(8,128)} copy(f32[50,128]{1,0:T(8,128)} %get-tuple-element.4) | data formatting | bytes 51200
  56.6 1.4 %copy.15 = f32[50,128]{1,0:T(8,128)} copy(f32[50,128]{1,0:T(8,128)} %get-tuple-element.5) | data formatting | bytes 51200

commit v2 on v1

--- a/solution.py
+++ b/solution.py
@@ -14,10 +14,13 @@
 NZ = 16
 NP = 32
 NY = 4
-ROWS = 56
+ROWS = 50
 PARTS = (2, 1, 3, 0)
-VIA = ((3, 8), (-3, -7), (2, 7), (-2, -6), (1, 6), (-1, -5))
-LAST = (4, -3, 3, -2, 2, -1, 1, 5, -4)
+HOPS = (
+    ((2, 8), (1, 7), (-1, -7)),
+    ((2, 5), (1, 4), (-2, -5), (-1, -4), (3, 6), (-3, -6)),
+    ((2, 2), (1, 1), (-2, -2), (-1, -1), (3, 3), (-3, -3)),
+)
 
 
 def halves(value):
@@ -70,8 +73,7 @@
     outbox,
     inbox,
     chunks,
-    via_in,
-    last_in,
+    hop_in,
     group,
     group_pos,
     seats_to_pos,
@@ -85,10 +87,8 @@
     load_sem,
     plane_send,
     plane_recv,
-    via_send,
-    via_recv,
-    last_send,
-    last_recv,
+    hop_send,
+    hop_recv,
     group_send,
     group_recv,
     pos_send,
@@ -141,7 +141,7 @@
 
     barrier = pltpu.get_barrier_semaphore()
 
-    for step in (5, 11, 4, 12, 3, 13, 2, 14, 1, 15):
+    for step in (3, 13, 2, 14, 1, 15):
         pl.semaphore_signal(barrier, inc=1, device_id=ring_peer(step), device_id_type=MESH)
 
     def plane_steps(part, body):
@@ -239,7 +239,7 @@
         rows = rows[:, :128] + rows[:, 128:]
         outbox[part * 8 : (part + 1) * 8] = rows.reshape(8, 4, 8, 128)
 
-    pl.semaphore_wait(barrier, 43)
+    pl.semaphore_wait(barrier, 39)
     loads[5].wait()
 
     group_pos[0] = jnp.broadcast_to(positions[...], (8, 128))
@@ -341,47 +341,46 @@
     def chunk_of(relative):
         return (relative + 11) % 16
 
-    def via_copy(n):
-        step, relative = VIA[n]
+    def hop_copy(hop, n):
+        step, relative = HOPS[hop][n]
         return pltpu.make_async_remote_copy(
             src_ref=chunks.at[chunk_of(relative), pl.ds(0, ROWS)],
-            dst_ref=via_in.at[n],
-            send_sem=via_send.at[n],
-            recv_sem=via_recv.at[n],
+            dst_ref=hop_in.at[hop, n],
+            send_sem=hop_send.at[hop, n],
+            recv_sem=hop_recv.at[hop, n],
             device_id=ring_peer(step % NZ),
             device_id_type=MESH,
         )
 
-    def last_copy(n):
-        relative = LAST[n]
-        return pltpu.make_async_remote_copy(
-            src_ref=chunks.at[chunk_of(relative), pl.ds(0, ROWS)],
-            dst_ref=last_in.at[n],
-            send_sem=last_send.at[n],
-            recv_sem=last_recv.at[n],
-            device_id=ring_peer(relative % NZ),
-            device_id_type=MESH,
-        )
+    def add_up(hop, members, relative):
+        for n in members:
+            hop_copy(hop, n).wait_recv()
+        added = hop_in[hop, members[0]]
+        for n in members[1:]:
+            added = added + hop_in[hop, n]
+        chunks[chunk_of(relative), 0:ROWS, :] += added
 
     wait_plane(0, plane_recv)
     gather(0)
-    for n in (0, 2, 4):
-        via_copy(n).start()
+    for hop, n in ((0, 0), (0, 1), (1, 0)):
+        hop_copy(hop, n).start()
     gather(1)
-    for n in (1, 3, 5):
-        via_copy(n).start()
+    for hop, n in ((0, 2), (1, 2), (1, 3)):
+        hop_copy(hop, n).start()
     wait_plane(1, plane_recv)
+    gather(3)
+    hop_copy(1, 1).start()
+    add_up(0, (0, 1), 6)
+    hop_copy(1, 4).start()
+    add_up(0, (2,), -6)
+    hop_copy(1, 5).start()
     gather(2)
-    gather(3)
-    for n in range(7):
-        last_copy(n).start()
-    for n in range(6):
-        via_copy(n).wait_recv()
-    for first, relative in ((0, 5), (1, -4)):
-        added = via_in[first] + via_in[first + 2] + via_in[first + 4]
-        chunks[chunk_of(relative), 0:ROWS, :] += added
-    for n in (7, 8):
-        last_copy(n).start()
+    for n in range(4):
+        hop_copy(2, n).start()
+    add_up(1, (0, 1, 4), 3)
+    hop_copy(2, 4).start()
+    add_up(1, (2, 3, 5), -3)
+    hop_copy(2, 5).start()
     def group_copy(step):
         return pltpu.make_async_remote_copy(
             src_ref=group.at[0],
@@ -392,18 +391,15 @@
             device_id_type=MESH,
         )
 
-    mine = chunks[chunk_of(0), 0:ROWS, :]
-    for n in range(9):
-        last_copy(n).wait_recv()
-        mine = mine + last_in[n]
-    group[0] = mine
+    add_up(2, (0, 1, 2, 3, 4, 5), 0)
+    group[0] = chunks[chunk_of(0), 0:ROWS, :]
     for step in (2, 1, 3):
         group_copy(step).start()
     for load in loads[8:]:
         load.wait()
     for step in (1, 3, 2):
         group_copy(step).wait_recv()
-    blank = jnp.zeros((8, 128), F32)
+    blank = jnp.zeros((14, 128), F32)
     wide = jnp.concatenate(
         [jnp.concatenate([group[step], blank], axis=0) for step in range(NY)], axis=1
     )
@@ -474,10 +470,9 @@
 
     for half in range(2):
         wait_plane(half, plane_send)
-    for n in range(6):
-        via_copy(n).wait_send()
-    for n in range(9):
-        last_copy(n).wait_send()
+    for hop in range(3):
+        for n in range(len(HOPS[hop])):
+            hop_copy(hop, n).wait_send()
     for step in range(1, NY):
         pos_copy(step).wait_send()
         group_copy(step).wait_send()
@@ -526,8 +521,7 @@
             pltpu.VMEM((NP, 4, 8, 128), F32),
             pltpu.VMEM((4, NP, 8, 128), F32),
             pltpu.VMEM((NZ, 64, 128), F32),
-            pltpu.VMEM((6, ROWS, 128), F32),
-            pltpu.VMEM((9, ROWS, 128), F32),
+            pltpu.VMEM((3, 6, ROWS, 128), F32),
             pltpu.VMEM((NY, ROWS, 128), F32),
             pltpu.VMEM((NY, 8, 128), jnp.int32),
             pltpu.VMEM((128, 512), BF16),
@@ -541,10 +535,8 @@
             dma((10,)),
             dma((2,)),
             dma((2,)),
-            dma((6,)),
-            dma((6,)),
-            dma((9,)),
-            dma((9,)),
+            dma((3, 6)),
+            dma((3, 6)),
             dma((NY,)),
             dma((NY,)),
             dma((NY,)),

time: 58.3 us -> 55.1 us (0.945)
  Pallas kernels: 54.6 us -> 51.5 us
    pallas_call x1, Pallas kernels: 54.6 us -> 51.5 us  [per_device(): pl.pallas_call(kernel, out_shape=(jax.ShapeDtypeStruct((50, 128), F32), j...]
where the time goes in v2:
time: 55.1 us; the launch traced here: 54.8 us
  Pallas kernels  51.5 us (93%)
  local copies, waits for them, and re-layouts  2.72 us (5%)
  between operations  0.64 us (1%)
    pallas_call x1, Pallas kernels, per_device(): pl.pallas_call(kernel, out_shape=(jax.ShapeDtypeStruct((50, 128), F32), j...  51.5 us
    unnamed x2, local copies, waits for them, and re-layouts  2.72 us

profile of v2, /device:TPU:6, one launch (start us, length us, event | category | flops | bytes accessed | tf_op | source)
XLA Modules:
  0.0 54.8 jit_solution(6352736013940050153)
XLA Ops:
  0.6 51.5 %shard_map.113 = (f32[50,128]{1,0:T(8,128)}, f32[50,128]{1,0:T(8,128)}) custom-call(f32[5,35,256]{2,1,0:T(8,128)} %bitcast.9, f32[35,64]{1,0:T(8,128)} %bitcast.11, f32[10,64,256]{2,1,0:T(8,128)} %bitcast.8, s32[4,256]{1,0:T(4,128)} %bitcast.13, s32[4,256]{1,0:T(4,128)} %bitcast.14, s32[1,128]{1,0:T(1,128)} %bitcast.15, f32[50,50,128]{2,1,0:T(8,128)} %inverse_hbm.1, ...), custom_call_target="tpu_custom_call" | custom-call | tf_op jit(solution)/shard_map/pallas_call | solution.py:499
  52.1 1.4 %copy.14 = f32[50,128]{1,0:T(8,128)} copy(f32[50,128]{1,0:T(8,128)} %get-tuple-element.4) | data formatting | bytes 51200
  53.5 1.4 %copy.15 = f32[50,128]{1,0:T(8,128)} copy(f32[50,128]{1,0:T(8,128)} %get-tuple-element.5) | data formatting | bytes 51200

commit v3 on v2

--- a/solution.py
+++ b/solution.py
@@ -55,8 +55,7 @@
     jacobian_hbm,
     lift_hbm,
     offsets_hbm,
-    coarse_out,
-    correction_out,
+    result,
     residual,
     fine_basis,
     basis,
@@ -406,7 +405,7 @@
     high, low = halves(wide)
     coarse = dot_nt(jnp.concatenate([high, low], axis=0), seats_to_pos[...])
     coarse = (coarse[:64] + coarse[64:])[:50]
-    coarse_out[...] = coarse
+    result[0, 0:50, :] = coarse
 
     def apply_inverse(field):
         return jnp.sum(inverse[...] * field[None], axis=1)
@@ -442,31 +441,39 @@
             parts.append(jnp.where(lane_part == 3, low_rows, jnp.where(lane_part == 0, high_rows, F32(0.0))))
         return jnp.concatenate(parts, axis=0)
 
-    field = apply_inverse(coarse)
     tail = jnp.zeros((14, 128), F32)
-    for it in range(2):
-        whole = jnp.concatenate([field, tail], axis=0)
-        ends_high[it] = packed(whole, 3)
-        ends_low[it] = packed(whole, 0)
-        halo_copy(it, True).start()
-        halo_copy(it, False).start()
-        halo_copy(it, True).wait_recv()
-        halo_copy(it, False).wait_recv()
-        wide = jnp.concatenate([whole, unpacked(halo_low[it], halo_high[it])], axis=1)
-        high, low = halves(wide)
-        picked = dot_nn(jnp.concatenate([high, low], axis=0), chooser[...]).astype(BF16)
-        lifted = []
-        for f in range(4):
-            both = dot_nn(lift_rows[f], picked[:, f * 128 : f * 128 + 128])
-            lifted.append(both[:80] + both[80:])
-        for w in range(5):
-            total = jnp.zeros((16, 128), F32)
+    coupling[0:50, :] = jnp.zeros((50, 128), F32)
+
+    def sweep(it, carry):
+        field = apply_inverse(result[0, 0:50, :] - coupling[0:50, :])
+        result[1, 0:50, :] = field
+
+        @pl.when(it < 2)
+        def _():
+            whole = jnp.concatenate([field, tail], axis=0)
+            ends_high[it] = packed(whole, 3)
+            ends_low[it] = packed(whole, 0)
+            halo_copy(it, True).start()
+            halo_copy(it, False).start()
+            halo_copy(it, True).wait_recv()
+            halo_copy(it, False).wait_recv()
+            wide = jnp.concatenate([whole, unpacked(halo_low[it], halo_high[it])], axis=1)
+            high, low = halves(wide)
+            picked = dot_nn(jnp.concatenate([high, low], axis=0), chooser[...]).astype(BF16)
+            lifted = []
             for f in range(4):
-                for v in range(5):
-                    total = total + lifted[f][v * 16 : v * 16 + 16] * jacobian[w, v, f : f + 1, :]
-            coupling[pl.ds(w, 10, stride=5), :] = total[:10]
-        field = apply_inverse(coarse - coupling[0:50, :])
-    correction_out[...] = field
+                both = dot_nn(lift_rows[f], picked[:, f * 128 : f * 128 + 128])
+                lifted.append(both[:80] + both[80:])
+            for w in range(5):
+                total = jnp.zeros((16, 128), F32)
+                for f in range(4):
+                    for v in range(5):
+                        total = total + lifted[f][v * 16 : v * 16 + 16] * jacobian[w, v, f : f + 1, :]
+                coupling[pl.ds(w, 10, stride=5), :] = total[:10]
+
+        return carry
+
+    lax.fori_loop(0, 3, sweep, 0)
 
     for half in range(2):
         wait_plane(half, plane_send)
@@ -496,14 +503,11 @@
     vmem = pl.BlockSpec(memory_space=pltpu.VMEM)
     hbm = pl.BlockSpec(memory_space=pl.ANY)
     dma = pltpu.SemaphoreType.DMA
-    return pl.pallas_call(
+    result = pl.pallas_call(
         kernel,
-        out_shape=(
-            jax.ShapeDtypeStruct((50, 128), F32),
-            jax.ShapeDtypeStruct((50, 128), F32),
-        ),
+        out_shape=jax.ShapeDtypeStruct((2, 56, 128), F32),
         in_specs=[hbm] * 10,
-        out_specs=(vmem, vmem),
+        out_specs=vmem,
         scratch_shapes=[
             pltpu.VMEM((5, 35, 256), F32),
             pltpu.VMEM((35, 64), F32),
@@ -559,6 +563,7 @@
         face_lift.transpose(1, 0, 2),
         face_offset,
     )
+    return result[0, :50], result[1, :50]
 
 
 def solution(mesh):

time: 55.1 us -> 53.8 us (0.976)
  local copies, waits for them, and re-layouts: 2.72 us -> 1.39 us
    unnamed x2 -> x0, local copies, waits for them, and re-layouts: 2.72 us -> none
    squeeze x0 -> x1, local copies, waits for them, and re-layouts: none -> 1.39 us  [per_device(): return (result[0, :50], result[1, :50])]
where the time goes in v3:
time: 53.8 us; the launch traced here: 53.6 us
  Pallas kernels  51.6 us (96%)
  local copies, waits for them, and re-layouts  1.39 us (3%)
  between operations  0.64 us (1%)
    pallas_call x1, Pallas kernels, per_device(): pl.pallas_call(kernel, out_shape=jax.ShapeDtypeStruct((2, 56, 128), F32),...  51.6 us
    squeeze x1, local copies, waits for them, and re-layouts, per_device(): return (result[0, :50], result[1, :50])  1.39 us

profile of v3, /device:TPU:6, one launch (start us, length us, event | category | flops | bytes accessed | tf_op | source)
XLA Modules:
  0.0 53.6 jit_solution(8412223930342656294)
XLA Ops:
  0.6 51.6 %shard_map.113 = f32[2,56,128]{2,1,0:T(8,128)} custom-call(f32[5,35,256]{2,1,0:T(8,128)} %bitcast.13, f32[35,64]{1,0:T(8,128)} %bitcast.15, f32[10,64,256]{2,1,0:T(8,128)} %bitcast.12, s32[4,256]{1,0:T(4,128)} %bitcast.17, s32[4,256]{1,0:T(4,128)} %bitcast.18, s32[1,128]{1,0:T(1,128)} %bitcast.19, f32[50,50,128]{2,1,0:T(8,128)} %inverse_hbm.1, ...), custom_call_target="tpu_custom_call" | custom-call | tf_op jit(solution)/shard_map/pallas_call | solution.py:506
  52.2 1.4 %slice_bitcast_fusion = (f32[50,128]{1,0:T(8,128)}, f32[50,128]{1,0:T(8,128)}) fusion(f32[2,56,128]{2,1,0:T(8,128)} %shard_map.113), kind=kLoop, calls=%fused_computation | loop fusion | bytes 102400 | tf_op jit(solution)/shard_map/squeeze | solution.py:566

commit v4 on v3

--- a/solution.py
+++ b/solution.py
@@ -302,14 +302,6 @@
             wide = dot_nn(dot_nn(take_a, part).astype(BF16), take_b)
             wide = jnp.where(same, wide, F32(0.0)).astype(BF16)
             lift_rows[f, n * 80 : n * 80 + 80, :] = jnp.concatenate([wide, wide], axis=1)
-    for step in range(1, NY):
-        pos_copy(step).wait_recv()
-    place = iota((128, 128), 0) + block * 128
-    for step in range(NY):
-        seats_to_pos[:, step * 128 : step * 128 + 128] = ones_where(
-            place == group_pos[step, 0:1, :]
-        ).astype(BF16)
-
     def wait_plane(half, sems):
         whole = inbox.at[pl.ds(half * 2, 2), pl.ds(1, NP - 1)]
         pltpu.make_async_copy(whole, whole, sems.at[half]).wait()
@@ -369,6 +361,14 @@
     wait_plane(1, plane_recv)
     gather(3)
     hop_copy(1, 1).start()
+    for step in range(1, NY):
+        pos_copy(step).wait_recv()
+    place = iota((128, 128), 0) + block * 128
+    for step in range(NY):
+        seats_to_pos[:, step * 128 : step * 128 + 128] = ones_where(
+            place == group_pos[step, 0:1, :]
+        ).astype(BF16)
+
     add_up(0, (0, 1), 6)
     hop_copy(1, 4).start()
     add_up(0, (2,), -6)

time: 53.8 us -> 52.9 us (0.983); the launches traced: 53.6 us -> 51.9 us
  Pallas kernels: 51.6 us -> 49.9 us
    pallas_call x1, Pallas kernels: 51.6 us -> 49.9 us  [per_device(): pl.pallas_call(kernel, out_shape=jax.ShapeDtypeStruct((2, 56, 128), F32),...]
where the time goes in v4:
time: 52.9 us; the launch traced here: 51.9 us
  Pallas kernels  49.9 us (94%)
  local copies, waits for them, and re-layouts  1.39 us (3%)
  between operations  0.64 us (1%)
    pallas_call x1, Pallas kernels, per_device(): pl.pallas_call(kernel, out_shape=jax.ShapeDtypeStruct((2, 56, 128), F32),...  49.9 us
    squeeze x1, local copies, waits for them, and re-layouts, per_device(): return (result[0, :50], result[1, :50])  1.39 us

profile of v4, /device:TPU:6, one launch (start us, length us, event | category | flops | bytes accessed | tf_op | source)
XLA Modules:
  0.0 51.9 jit_solution(6721245029275085106)
XLA Ops:
  0.6 49.9 %shard_map.113 = f32[2,56,128]{2,1,0:T(8,128)} custom-call(f32[5,35,256]{2,1,0:T(8,128)} %bitcast.13, f32[35,64]{1,0:T(8,128)} %bitcast.15, f32[10,64,256]{2,1,0:T(8,128)} %bitcast.12, s32[4,256]{1,0:T(4,128)} %bitcast.17, s32[4,256]{1,0:T(4,128)} %bitcast.18, s32[1,128]{1,0:T(1,128)} %bitcast.19, f32[50,50,128]{2,1,0:T(8,128)} %inverse_hbm.1, ...), custom_call_target="tpu_custom_call" | custom-call | tf_op jit(solution)/shard_map/pallas_call | solution.py:506
  50.5 1.4 %slice_bitcast_fusion = (f32[50,128]{1,0:T(8,128)}, f32[50,128]{1,0:T(8,128)}) fusion(f32[2,56,128]{2,1,0:T(8,128)} %shard_map.113), kind=kLoop, calls=%fused_computation | loop fusion | bytes 102400 | tf_op jit(solution)/shard_map/squeeze | solution.py:566

commit v5 on v4

--- a/solution.py
+++ b/solution.py
@@ -241,7 +241,6 @@
     pl.semaphore_wait(barrier, 39)
     loads[5].wait()
 
-    group_pos[0] = jnp.broadcast_to(positions[...], (8, 128))
 
     def pos_copy(step):
         return pltpu.make_async_remote_copy(
@@ -266,6 +265,7 @@
     for half in range(2):
         for part in PARTS:
             plane_steps(part, lambda step, half=half: plane_copy(half, step).start())
+    group_pos[0] = jnp.broadcast_to(positions[...], (8, 128))
     for step in range(1, NY):
         pos_copy(step).start()
     inbox[:, 0] = outbox[0]
@@ -346,10 +346,7 @@
     def add_up(hop, members, relative):
         for n in members:
             hop_copy(hop, n).wait_recv()
-        added = hop_in[hop, members[0]]
-        for n in members[1:]:
-            added = added + hop_in[hop, n]
-        chunks[chunk_of(relative), 0:ROWS, :] += added
+            chunks[chunk_of(relative), 0:ROWS, :] += hop_in[hop, n]
 
     wait_plane(0, plane_recv)
     gather(0)
@@ -361,6 +358,7 @@
     wait_plane(1, plane_recv)
     gather(3)
     hop_copy(1, 1).start()
+    gather(2)
     for step in range(1, NY):
         pos_copy(step).wait_recv()
     place = iota((128, 128), 0) + block * 128
@@ -373,7 +371,6 @@
     hop_copy(1, 4).start()
     add_up(0, (2,), -6)
     hop_copy(1, 5).start()
-    gather(2)
     for n in range(4):
         hop_copy(2, n).start()
     add_up(1, (0, 1, 4), 3)

time: 52.9 us -> 53.1 us (level)
  the two profiles are of different devices: /device:TPU:6 before, /device:TPU:2 now
where the time goes in v5:
time: 53.1 us; the launch traced here: 52.9 us
  Pallas kernels  50.9 us (96%)
  local copies, waits for them, and re-layouts  1.39 us (3%)
  between operations  0.64 us (1%)
    pallas_call x1, Pallas kernels, per_device(): pl.pallas_call(kernel, out_shape=jax.ShapeDtypeStruct((2, 56, 128), F32),...  50.9 us
    squeeze x1, local copies, waits for them, and re-layouts, per_device(): return (result[0, :50], result[1, :50])  1.39 us

profile of v5, /device:TPU:2, one launch (start us, length us, event | category | flops | bytes accessed | tf_op | source)
XLA Modules:
  0.0 52.9 jit_solution(5261142506981823933)
XLA Ops:
  0.6 50.9 %shard_map.113 = f32[2,56,128]{2,1,0:T(8,128)} custom-call(f32[5,35,256]{2,1,0:T(8,128)} %bitcast.13, f32[35,64]{1,0:T(8,128)} %bitcast.15, f32[10,64,256]{2,1,0:T(8,128)} %bitcast.12, s32[4,256]{1,0:T(4,128)} %bitcast.17, s32[4,256]{1,0:T(4,128)} %bitcast.18, s32[1,128]{1,0:T(1,128)} %bitcast.19, f32[50,50,128]{2,1,0:T(8,128)} %inverse_hbm.1, ...), custom_call_target="tpu_custom_call" | custom-call | tf_op jit(solution)/shard_map/pallas_call | solution.py:503
  51.5 1.4 %slice_bitcast_fusion = (f32[50,128]{1,0:T(8,128)}, f32[50,128]{1,0:T(8,128)}) fusion(f32[2,56,128]{2,1,0:T(8,128)} %shard_map.113), kind=kLoop, calls=%fused_computation | loop fusion | bytes 102400 | tf_op jit(solution)/shard_map/squeeze | solution.py:563
